TPU v7x, 128 devices: a whole 4x4x4 slice. The times are simulated.
128 devices in a mesh: ka: 16 (over x_lo, z, core), aux: 8 (over x_hi, y).
Axes of the slice: x: 4 (x_hi: 2, x_lo: 2; x = x_hi * 2 + x_lo), y: 4, z: 4, core: 2. Of those that a mesh axis runs over, the one named last changes fastest.
Arguments:
- orbital_coef: bfloat16 [2, 16, 192, 128], P(None, 'ka'), may hold values from -0.4375 to 0.4375
- dftensor: bfloat16 [2, 16, 192, 192, 1024], P(None, 'ka', None, None, 'aux'), may hold values from -1.5 to 1.5
- shifted_index: int32 [16], replicated, may hold values from 0 to 15, each once
Outputs:
- integrals: float32 [2, 16384, 1024], P(None, 'ka', 'aux')
Inputs may be any that keep to these rules, and one draw needn't show every extreme that they name: `shifted_index`: a permutation of the 16 k-points.
All inputs are finite; a program needn't handle non-finite values.
Results may differ from a plain program's by a relative error of at most 0.004.
Values may be sent and summed in bfloat16 or wider, within the bound.
A program may use at most 192 MiB of HBM per device.

v0:
```python
import functools

import jax
import jax.numpy as jnp
from jax import lax
from jax.experimental import pallas as pl
from jax.experimental.pallas import tpu as pltpu
from jax.sharding import PartitionSpec as P

F32, BF16 = jnp.float32, jnp.bfloat16
MESH = pl.DeviceIdType.MESH
ROWS = 16
CHUNKS = 4
CORES, ZS, XS, YS = 2, 4, 2, 4


def matmul(left, right):
    return lax.dot_general(left, right, (((1,), (0,)), ((), ())), preferred_element_type=F32)


def matmul_nt(left, right):
    return lax.dot_general(left, right, (((1,), (1,)), ((), ())), preferred_element_type=F32)


def kernel(coef, tensor, index, out, blocks, w1, w2, half, cg, cs, away, mine, other, za, zb, zm, zp, xr, fg, cols,
           lsem, gsend, grecv, dsend, drecv, local_sem):
    nao = coef.shape[2]
    part = nao // YS
    nblocks = nao // ROWS
    ka, aux = lax.axis_index("ka"), lax.axis_index("aux")
    core, z, x = lax.rem(ka, CORES), lax.rem(lax.div(ka, CORES), ZS), lax.div(ka, CORES * ZS)
    y, xh = lax.rem(aux, YS), lax.div(aux, YS)
    up, down, across = lax.rem(z + 1, ZS), lax.rem(z + ZS - 1, ZS), lax.rem(z + 2, ZS)
    y_up, y_down = lax.rem(y + 1, YS), lax.rem(y + YS - 1, YS)
    aux_far = lax.rem(aux + YS, 2 * YS)
    to_core = (ka + 1 - 2 * core, aux)
    to_x = (lax.rem(ka + CORES * ZS, XS * CORES * ZS), aux)
    to_up = (x * CORES * ZS + up * CORES + core, aux)
    to_down = (x * CORES * ZS + down * CORES + core, aux)
    to_y_up, to_y_down = (ka, xh * YS + y_up), (ka, xh * YS + y_down)
    to_far = (ka, aux_far)
    x_other = 1 - x

    def load(i):
        return pltpu.make_async_copy(tensor.at[:, :, pl.ds(pl.multiple_of(i * ROWS, ROWS), ROWS), :], blocks.at[i], lsem.at[i])

    for i in range(nblocks):
        load(i).start()

    barrier = pltpu.get_barrier_semaphore()
    for partner in (to_core, to_x, to_up, to_down, to_y_up, to_y_down, to_far):
        pl.semaphore_signal(barrier, inc=1, device_id=partner, device_id_type=MESH)
    pl.semaphore_wait(barrier, 7)

    def send(src, dst, send_sem, recv_sem, where):
        return pltpu.make_async_remote_copy(
            src_ref=src, dst_ref=dst, send_sem=send_sem, recv_sem=recv_sem, device_id=where, device_id_type=MESH
        )

    slot = z * 4 + x * 2 + core
    own_rows = coef.at[:, 0, pl.ds(pl.multiple_of(y * part, 16), part), :]
    keep = pltpu.make_async_copy(own_rows, cg.at[slot], local_sem)

    def gather(n):
        def one(src, dst, where):
            return send(src, dst, gsend.at[n], grecv.at[n], where)

        if n == 0:
            return one(own_rows, cg.at[slot], to_core)
        if n == 1:
            rows = cg.at[pl.ds(z * 4 + x * 2, 2)]
            return one(rows, rows, to_x)
        if n in (2, 3):
            rows = cg.at[pl.ds(z * 4, 4)]
            return one(rows, rows, to_up if n == 2 else to_down)
        if n == 4:
            rows = cg.at[pl.ds(down * 4, 4)]
            return one(rows, rows, to_up)
        if n in (5, 6):
            return one(cs.at[y], cs.at[y], to_y_up if n == 5 else to_y_down)
        return one(cs.at[y_down], cs.at[y_down], to_y_up)

    keep.start()
    gather(0).start()

    left_real, left_imag = coef[0, 0], coef[1, 0]
    w1[...] = jnp.concatenate(
        [jnp.concatenate([left_real, -left_imag], 1), jnp.concatenate([left_imag, left_real], 1)], 0
    ).T

    def first(i, carry):
        @pl.when(i == 1)
        def _():
            keep.wait()
            gather(0).wait()
            gather(1).start()

        @pl.when(i == 3)
        def _():
            gather(1).wait()
            gather(2).start()
            gather(3).start()

        @pl.when(i == 6)
        def _():
            gather(2).wait()
            gather(3).wait()
            gather(4).start()

        @pl.when(i == 9)
        def _():
            gather(4).wait()
            wanted = index[ka]
            picked = lax.rem(lax.div(wanted, 2), 4) * 4 + lax.div(wanted, 8) * 2 + lax.rem(wanted, 2)
            cs[y] = cg[picked]
            gather(5).start()
            gather(6).start()

        load(i).wait()
        block = jnp.swapaxes(blocks[i].reshape(2 * nao, ROWS, 128), 0, 1)
        halves = []
        for n in range(0, ROWS, 2):
            got = matmul(w1[...], jnp.concatenate([block[n], block[n + 1]], 1)).astype(BF16)
            halves += [got[:, :128], got[:, 128:]]
        half[:, pl.ds(pl.multiple_of(i * ROWS, ROWS), ROWS), :] = jnp.swapaxes(jnp.stack(halves), 0, 1)
        return carry

    lax.fori_loop(0, nblocks, first, 0)

    gather(5).wait()
    gather(6).wait()
    gather(7).start()
    gather(7).wait()
    right_real = jnp.concatenate([cs[n, 0] for n in range(YS)], 0)
    right_imag = jnp.concatenate([cs[n, 1] for n in range(YS)], 0)
    w2[...] = jnp.concatenate(
        [jnp.concatenate([right_real, right_imag], 1), jnp.concatenate([-right_imag, right_real], 1)], 0
    ).T

    def pairs(c, target, into):
        def one(q, carry):
            a = 8 * (lax.rem(q, 2) * 8 + lax.div(q, 2) * 2 + target) + 2 * c
            sides = [jnp.concatenate([half[a + n], half[128 + a + n]], 0) for n in range(2)]
            got = matmul(w2[...], jnp.concatenate(sides, 1)).astype(BF16)
            into[c, q, 0] = got[:, :128]
            into[c, q, 1] = got[:, 128:]
            return carry

        lax.fori_loop(0, 8, one, 0)

    def add(dst, srcs, scale=None):
        def one(i, carry):
            at = (lax.div(i, 4), pl.ds(pl.multiple_of(lax.rem(i, 4) * 64, 64), 64))
            total = srcs[0][at].astype(F32)
            for src in srcs[1:]:
                total = total + src[at].astype(F32)
            if scale is not None:
                total = total * scale
            dst[at] = total.astype(BF16)
            return carry

        lax.fori_loop(0, 8, one, 0)

    def move(kind, c):
        def one(src, dst, where):
            return send(src, dst, dsend.at[kind, c], drecv.at[kind, c], where)

        if kind == 0:
            return one(away.at[c], other.at[c], to_core)
        if kind == 1:
            return one(mine.at[c, across * 2], za.at[c], to_up)
        if kind == 2:
            return one(mine.at[c, across * 2 + 1], zb.at[c], to_down)
        if kind in (3, 5):
            n = 1 if kind == 3 else 0
            return one(mine.at[c, up * 2 + n], zm.at[c, n], to_up)
        if kind in (4, 6):
            n = 0 if kind == 4 else 1
            return one(mine.at[c, down * 2 + n], zp.at[c, n], to_down)
        if kind == 7:
            return one(mine.at[c, z * 2 + x_other], xr.at[c], to_x)
        if kind == 8:
            return one(fg.at[aux, c], fg.at[aux, c], to_far)
        if kind in (9, 10):
            return one(fg.at[aux, c], fg.at[aux, c], to_y_up if kind == 9 else to_y_down)
        if kind in (11, 12):
            return one(fg.at[aux_far, c], fg.at[aux_far, c], to_y_up if kind == 11 else to_y_down)
        base = (xh if kind < 15 else 1 - xh) * YS
        if kind in (13, 15):
            piece = fg.at[base + y_down, c, 0]
            return one(piece, piece, to_y_up)
        piece = fg.at[base + y_up, c, 1]
        return one(piece, piece, to_y_down)

    def stage_a(c):
        pairs(c, 1 - core, away)
        move(0, c).start()
        pairs(c, core, mine)
        move(0, c).wait_recv()
        for kind, q in ((1, across * 2), (2, across * 2 + 1)):
            add(mine.at[c, q], (mine.at[c, q], other.at[c, q]))
            move(kind, c).start()

    def stage_a2(c):
        for kind, q in ((3, up * 2 + 1), (4, down * 2)):
            add(mine.at[c, q], (mine.at[c, q], other.at[c, q]))
            move(kind, c).start()

    def stage_b(c):
        for first_kind, kind, q, got in ((1, 5, up * 2, za), (2, 6, down * 2 + 1, zb)):
            move(first_kind, c).wait_recv()
            add(mine.at[c, q], (mine.at[c, q], other.at[c, q], got.at[c]))
            move(kind, c).start()

    def stage_d(c):
        for kind in (3, 4, 5, 6):
            move(kind, c).wait_recv()
        q = z * 2 + x_other
        add(mine.at[c, q], (mine.at[c, q], other.at[c, q], zm.at[c, x_other], zp.at[c, x_other]))
        move(7, c).start()

    def stage_e(c):
        move(7, c).wait_recv()
        q = z * 2 + x
        add(fg.at[aux, c], (mine.at[c, q], other.at[c, q], zm.at[c, x], zp.at[c, x], xr.at[c]), 1 / (CORES * ZS * XS))
        for kind in (8, 9, 10):
            move(kind, c).start()

    def stage_g(c):
        move(8, c).wait_recv()
        move(11, c).start()
        move(12, c).start()

    def stage_h(c):
        for wait_kind, kind in ((9, 13), (10, 14), (11, 15), (12, 16)):
            move(wait_kind, c).wait_recv()
            move(kind, c).start()

    def stage_i(c):
        for kind in (13, 14, 15, 16):
            move(kind, c).wait_recv()

    stage_a(0)
    stage_a(1)
    stage_a2(0)
    stage_b(0)
    stage_a(2)
    stage_a2(1)
    stage_b(1)
    stage_a(3)
    stage_d(0)
    stage_a2(2)
    stage_b(2)
    stage_d(1)
    stage_e(0)
    stage_a2(3)
    stage_b(3)
    stage_g(0)
    stage_d(2)
    stage_e(1)
    stage_h(0)
    stage_g(1)
    stage_d(3)
    stage_e(2)
    stage_h(1)
    stage_g(2)
    stage_e(3)
    stage_h(2)
    stage_g(3)
    stage_h(3)
    for c in range(CHUNKS):
        stage_i(c)

    col_chunk, col_part = lax.div(aux, 2), lax.rem(aux, 2)
    for j in range(2 * YS):
        column = fg[j, col_chunk, col_part]
        real, imag = column[:128], column[128:]
        cols[j] = jnp.concatenate(
            [jnp.concatenate([real, imag], 1), jnp.concatenate([-imag, real], 1)], 0
        )

    def tile(c, carry):
        total = jnp.zeros((256, 256), F32)
        for j in range(2 * YS):
            rows = jnp.concatenate(
                [jnp.concatenate([fg[j, c, n, :128], fg[j, c, n, 128:]], 1) for n in range(2)], 0
            )
            total = total + matmul_nt(rows, cols[j])
        at = pl.ds(pl.multiple_of(c * 256, 256), 256)
        out[0, at, :] = total[:, :128]
        out[1, at, :] = total[:, 128:]
        return carry

    lax.fori_loop(0, CHUNKS, tile, 0)

    for kind in range(17):
        for c in range(CHUNKS):
            move(kind, c).wait_send()


def local(orbital_coef, dftensor, shifted_index):
    nao, nemb = orbital_coef.shape[2:]
    depth = dftensor.shape[-1]
    tensor = dftensor.reshape(2, nao, nao, depth)
    unit = (2, 2 * nemb, depth)
    return pl.pallas_call(
        kernel,
        out_shape=jax.ShapeDtypeStruct((2, 8 * nemb, nemb), F32),
        in_specs=[
            pl.BlockSpec(memory_space=pltpu.VMEM),
            pl.BlockSpec(memory_space=pl.ANY),
            pl.BlockSpec(memory_space=pltpu.SMEM),
        ],
        out_specs=pl.BlockSpec(memory_space=pltpu.VMEM),
        scratch_shapes=[
            pltpu.VMEM((nao // ROWS, 2, nao, ROWS, depth), BF16),
            pltpu.VMEM((2 * nemb, 2 * nao), BF16),
            pltpu.VMEM((2 * nemb, 2 * nao), BF16),
            pltpu.VMEM((2 * nemb, nao, depth), BF16),
            pltpu.VMEM((CORES * ZS * XS, 2, nao // YS, nemb), BF16),
            pltpu.VMEM((YS, 2, nao // YS, nemb), BF16),
            pltpu.VMEM((CHUNKS, ZS * XS) + unit, BF16),
            pltpu.VMEM((CHUNKS, ZS * XS) + unit, BF16),
            pltpu.VMEM((CHUNKS, ZS * XS) + unit, BF16),
            pltpu.VMEM((CHUNKS,) + unit, BF16),
            pltpu.VMEM((CHUNKS,) + unit, BF16),
            pltpu.VMEM((CHUNKS, XS) + unit, BF16),
            pltpu.VMEM((CHUNKS, XS) + unit, BF16),
            pltpu.VMEM((CHUNKS,) + unit, BF16),
            pltpu.VMEM((2 * YS, CHUNKS) + unit, BF16),
            pltpu.VMEM((2 * YS, 2 * nemb, 2 * depth), BF16),
            pltpu.SemaphoreType.DMA((nao // ROWS,)),
            pltpu.SemaphoreType.DMA((8,)),
            pltpu.SemaphoreType.DMA((8,)),
            pltpu.SemaphoreType.DMA((17, CHUNKS)),
            pltpu.SemaphoreType.DMA((17, CHUNKS)),
            pltpu.SemaphoreType.DMA,
        ],
        compiler_params=pltpu.CompilerParams(
            collective_id=0, has_side_effects=True, vmem_limit_bytes=66_000_000
        ),
    )(orbital_coef, tensor, shifted_index)


def solution(mesh):
    placed = (P(None, "ka", None, None), P(None, "ka", None, None, "aux"), P())
    return jax.shard_map(
        local, mesh=mesh, in_specs=placed, out_specs=P(None, "ka", "aux"), check_vma=False
    )
```

profile of v0, /device:TPU:0, one launch (start us, length us, event | category | flops | bytes accessed | tf_op | source)
XLA Modules:
  0.0 101.6 jit_solution(3140396439272050430)
XLA Ops:
  0.0 99.4 %shard_map.37 = f32[2,1024,128]{2,1,0:T(8,128)} custom-call(bf16[2,1,192,128]{3,2,1,0:T(8,128)(2,1)} %coef.1, bf16[2,192,192,128]{3,2,1,0:T(8,128)(2,1)} %bitcast.1, s32[16]{0:T(128)} %index.1), custom_call_target="tpu_custom_call" | custom-call | tf_op jit(solution)/shard_map/pallas_call | solution.py:306
  99.4 2.3 %copy.5 = f32[2,1024,128]{2,1,0:T(8,128)} copy(f32[2,1024,128]{2,1,0:T(8,128)} %shard_map.37) | data formatting | bytes 2097152
where the time goes:
time: 102 us
  Pallas kernels  99.4 us (97%)
  local copies, waits for them, and re-layouts  2.26 us (2%)
    pallas_call x1, Pallas kernels, local(): pl.pallas_call(kernel, out_shape=jax.ShapeDtypeStruct((2, 8 * nemb, nemb)...  99.4 us
    unnamed x1, local copies, waits for them, and re-layouts  2.26 us

commit v1 on v0

v1 whole, which is shorter than its diff:
```python
import functools

import jax
import jax.numpy as jnp
from jax import lax
from jax.experimental import pallas as pl
from jax.experimental.pallas import tpu as pltpu
from jax.sharding import PartitionSpec as P

F32, BF16 = jnp.float32, jnp.bfloat16
MESH = pl.DeviceIdType.MESH
ROWS = 16
CHUNKS = 8
SLOTS = 3
PICK_AT = 8
UNROLL = 4
CORES, ZS, XS, YS = 2, 4, 2, 4
NKA = CORES * ZS * XS
KINDS = 20


def matmul(left, right):
    return lax.dot_general(left, right, (((1,), (0,)), ((), ())), preferred_element_type=F32)


def matmul_nt(left, right):
    return lax.dot_general(left, right, (((1,), (1,)), ((), ())), preferred_element_type=F32)


def kernel(coef, tensor, index, out, blocks, turned, raw, w1f, w1, w2, half, cg, cs, away, mine, other, za, zb, zm, zp, xr, ra, rb, fg, cols,
           lsem, gsend, grecv, dsend, drecv, local_sem):
    nao = coef.shape[2]
    part = nao // YS
    nblocks = nao // ROWS
    ka, aux = lax.axis_index("ka"), lax.axis_index("aux")
    core, z, x = lax.rem(ka, CORES), lax.rem(lax.div(ka, CORES), ZS), lax.div(ka, CORES * ZS)
    y, xh = lax.rem(aux, YS), lax.div(aux, YS)
    up, down, across = lax.rem(z + 1, ZS), lax.rem(z + ZS - 1, ZS), lax.rem(z + 2, ZS)
    y_up, y_down = lax.rem(y + 1, YS), lax.rem(y + YS - 1, YS)
    aux_far = lax.rem(aux + YS, 2 * YS)
    to_core = (ka + 1 - 2 * core, aux)
    to_x = (lax.rem(ka + CORES * ZS, XS * CORES * ZS), aux)
    to_up = (x * CORES * ZS + up * CORES + core, aux)
    to_down = (x * CORES * ZS + down * CORES + core, aux)
    to_y_up, to_y_down = (ka, xh * YS + y_up), (ka, xh * YS + y_down)
    to_out = (lax.rem(ka + CORES * ZS, XS * CORES * ZS), aux_far)
    x_other = 1 - x

    def load(i):
        return pltpu.make_async_copy(tensor.at[:, :, pl.ds(pl.multiple_of(i * ROWS, ROWS), ROWS), :], blocks.at[lax.rem(i, SLOTS)], lsem.at[lax.rem(i, SLOTS)])

    for i in range(SLOTS - 1):
        load(i).start()

    barrier = pltpu.get_barrier_semaphore()
    to_ka = [(lax.rem(ka + n, NKA), aux) for n in range(1, NKA)]
    to_ys = [(ka, xh * YS + lax.rem(y + n, YS)) for n in range(1, YS)]
    partners = to_ka + to_ys + [to_out]
    for partner in partners:
        pl.semaphore_signal(barrier, inc=1, device_id=partner, device_id_type=MESH)

    def send(src, dst, send_sem, recv_sem, where):
        return pltpu.make_async_remote_copy(
            src_ref=src, dst_ref=dst, send_sem=send_sem, recv_sem=recv_sem, device_id=where, device_id_type=MESH
        )

    own_rows = coef.at[:, 0, pl.ds(pl.multiple_of(y * part, 16), part), :]
    keep = pltpu.make_async_copy(own_rows, cg.at[ka], local_sem)
    spread = [send(own_rows, cg.at[ka], gsend.at[n], grecv.at[n], where) for n, where in enumerate(to_ka)]
    collect = [
        send(cs.at[y], cs.at[y], gsend.at[NKA - 1 + n], grecv.at[NKA - 1 + n], where) for n, where in enumerate(to_ys)
    ]
    keep.start()
    left_real, left_imag = coef[0, 0], coef[1, 0]
    left = jnp.concatenate(
        [jnp.concatenate([left_real, -left_imag], 1), jnp.concatenate([left_imag, left_real], 1)], 0
    ).T.astype(F32)
    for k in range(3):
        w1f[k] = left[:, k * 128 : k * 128 + 128]
    for h in range(2):
        for n in range(8):
            rows = pl.ds((n // 4) * 128 + h * 4 + n % 4, 16, stride=8)
            w1[h, n * 16 : n * 16 + 16] = jnp.concatenate([w1f[k, rows, :] for k in range(3)], 1).astype(BF16)

    def transform(h, i):
        for n in range(0, ROWS, 2):
            got = matmul(w1[h], jnp.concatenate([turned[i, n], turned[i, n + 1]], 1)).astype(BF16)
            raw[n] = got[:, :128]
            raw[n + 1] = got[:, 128:]
        at = pl.ds(pl.multiple_of(i * ROWS, ROWS), ROWS)
        for m in range(0, 128, 16):
            half[h, m : m + 16, at, :] = jnp.swapaxes(raw[:, m : m + 16, :], 0, 1)

    def first(i, carry):
        @pl.when(i == PICK_AT)
        def _():
            keep.wait()
            for copy in spread:
                copy.wait()
            cs[y] = cg[index[ka]]
            for copy in collect:
                copy.start()

        @pl.when(i + SLOTS - 1 < nblocks)
        def _():
            load(i + SLOTS - 1).start()

        load(i).wait()
        for c in range(2):
            for m in range(0, nao, 16):
                piece = blocks[lax.rem(i, SLOTS), c, m : m + 16]
                turned[i, :, c * nao + m : c * nao + m + 16, :] = jnp.swapaxes(piece, 0, 1)
        transform(0, i)
        return carry

    first(0, 0)
    pl.semaphore_wait(barrier, len(partners))
    for copy in spread:
        copy.start()
    lax.fori_loop(1, nblocks, first, 0)

    for copy in collect:
        copy.wait()
    right_real = jnp.concatenate([cs[n, 0] for n in range(YS)], 0)
    right_imag = jnp.concatenate([cs[n, 1] for n in range(YS)], 0)
    w2[...] = jnp.concatenate(
        [jnp.concatenate([right_real, right_imag], 1), jnp.concatenate([-right_imag, right_real], 1)], 0
    ).T

    def second(begin, end):
        def one(i, carry):
            transform(1, i)
            return carry

        lax.fori_loop(begin, end, one, 0)

    def pairs(cc, target, into):
        def one(q, carry):
            t = lax.rem(q, 2) * 8 + lax.div(q, 2) * 2 + target
            sides = []
            for c in (2 * cc, 2 * cc + 1):
                row = c % 4 * 16 + t
                sides.append(jnp.concatenate([half[c // 4, row], half[c // 4, 64 + row]], 0))
            got = matmul(w2[...], jnp.concatenate(sides, 1)).astype(into.dtype)
            into[2 * cc, q] = got[:, :128]
            into[2 * cc + 1, q] = got[:, 128:]
            return carry

        lax.fori_loop(0, 8, one, 0, unroll=UNROLL)

    def add(dst, srcs, scale=None):
        def one(i, carry):
            at = pl.ds(pl.multiple_of(i * 64, 64), 64)
            total = srcs[0][at]
            for src in srcs[1:]:
                total = total + src[at].astype(F32)
            if scale is not None:
                total = total * scale
            dst[at] = total.astype(BF16)
            return carry

        lax.fori_loop(0, 4, one, 0)

    def move(kind, c):
        def one(src, dst, where):
            return send(src, dst, dsend.at[kind, c], drecv.at[kind, c], where)

        if kind == 0:
            both = pl.ds(2 * c, 2)
            return one(away.at[both], other.at[both], to_core)
        if kind == 1:
            return one(other.at[c, across * 2], za.at[c], to_up)
        if kind == 2:
            return one(other.at[c, across * 2 + 1], zb.at[c], to_down)
        if kind in (3, 5):
            n = 1 if kind == 3 else 0
            return one(other.at[c, up * 2 + n], zm.at[c, n], to_up)
        if kind in (4, 6):
            n = 0 if kind == 4 else 1
            return one(other.at[c, down * 2 + n], zp.at[c, n], to_down)
        if kind == 7:
            return one(other.at[c, z * 2 + x_other], xr.at[c], to_x)
        low, high = pl.ds(0, 128), pl.ds(128, 128)
        if kind == 8:
            return one(fg.at[aux, c, low], ra.at[c], to_x)
        if kind == 17:
            return one(fg.at[aux, c, high], rb.at[c], to_out)
        if kind == 18:
            return one(ra.at[c], fg.at[aux, c, low], to_out)
        if kind == 19:
            return one(rb.at[c], fg.at[aux_far, c, high], to_x)
        if kind in (9, 10):
            return one(fg.at[aux, c], fg.at[aux, c], to_y_up if kind == 9 else to_y_down)
        if kind in (11, 12):
            return one(fg.at[aux_far, c], fg.at[aux_far, c], to_y_up if kind == 11 else to_y_down)
        base = (xh if kind < 15 else 1 - xh) * YS
        if kind in (13, 15):
            piece = fg.at[base + y_down, c, low]
            return one(piece, piece, to_y_up)
        piece = fg.at[base + y_up, c, high]
        return one(piece, piece, to_y_down)

    def pair_away(cc):
        pairs(cc, 1 - core, away)
        move(0, cc).start()

    def pair_mine(cc):
        pairs(cc, core, mine)

    def wait_core(cc):
        move(0, cc).wait_recv()

    def stage_a(c):
        for kind, q in ((1, across * 2), (2, across * 2 + 1)):
            add(other.at[c, q], (mine.at[c, q], other.at[c, q]))
            move(kind, c).start()

    def stage_a2(c):
        for kind, q in ((3, up * 2 + 1), (4, down * 2)):
            add(other.at[c, q], (mine.at[c, q], other.at[c, q]))
            move(kind, c).start()

    def stage_b(c):
        for first_kind, kind, q, got in ((1, 5, up * 2, za), (2, 6, down * 2 + 1, zb)):
            move(first_kind, c).wait_recv()
            add(other.at[c, q], (mine.at[c, q], other.at[c, q], got.at[c]))
            move(kind, c).start()

    def stage_d(c):
        for kind in (3, 4, 5, 6):
            move(kind, c).wait_recv()
        q = z * 2 + x_other
        add(other.at[c, q], (mine.at[c, q], other.at[c, q], zm.at[c, x_other], zp.at[c, x_other]))
        move(7, c).start()

    def stage_e(c):
        move(7, c).wait_recv()
        q = z * 2 + x
        add(fg.at[aux, c], (mine.at[c, q], other.at[c, q], zm.at[c, x], zp.at[c, x], xr.at[c]), 1 / (CORES * ZS * XS))
        for kind in (8, 17, 9, 10):
            move(kind, c).start()

    def stage_r(c):
        for wait_kind, kind in ((8, 18), (17, 19)):
            move(wait_kind, c).wait_recv()
            move(kind, c).start()

    def stage_g(c):
        move(18, c).wait_recv()
        move(19, c).wait_recv()
        move(11, c).start()
        move(12, c).start()

    def stage_h(c):
        for wait_kind, kind in ((9, 13), (10, 14)):
            move(wait_kind, c).wait_recv()
            move(kind, c).start()

    def stage_h2(c):
        for wait_kind, kind in ((11, 15), (12, 16)):
            move(wait_kind, c).wait_recv()
            move(kind, c).start()

    def stage_i(c):
        for kind in (13, 14, 15, 16):
            move(kind, c).wait_recv()

    pair_away(0)
    pair_mine(0)
    second(0, 1)
    pair_away(1)
    pair_mine(1)
    wait_core(0)
    stage_a(0)
    stage_a(1)
    second(1, 3)
    stage_a2(0)
    second(3, 4)
    wait_core(1)
    second(4, 5)
    stage_a2(1)
    second(5, 6)
    stage_b(0)
    second(6, 8)
    stage_b(1)
    second(8, 12)
    stage_a(2)
    pair_away(2)
    stage_a2(2)
    pair_away(3)
    stage_d(0)
    pair_mine(2)
    stage_a(3)
    stage_d(1)
    pair_mine(3)
    wait_core(2)
    stage_a(4)
    stage_b(2)
    stage_e(0)
    wait_core(3)
    stage_a2(4)
    stage_e(1)
    stage_r(0)
    stage_a2(3)
    stage_b(3)
    stage_b(4)
    stage_h(0)
    stage_r(1)
    stage_d(2)
    stage_h(1)
    stage_g(0)
    stage_g(1)
    stage_a(5)
    stage_e(2)
    stage_a2(5)
    stage_h2(0)
    stage_d(3)
    stage_a(6)
    stage_h2(1)
    stage_d(4)
    stage_r(2)
    stage_a2(6)
    stage_h(2)
    stage_b(5)
    stage_e(3)
    stage_e(4)
    stage_a(7)
    stage_g(2)
    stage_b(6)
    stage_r(3)
    stage_h(3)
    stage_r(4)
    stage_a2(7)
    stage_h(4)
    stage_d(5)
    stage_g(3)
    stage_h2(2)
    stage_g(4)
    stage_b(7)
    stage_d(6)
    stage_e(5)
    stage_h2(3)
    stage_d(7)
    stage_h2(4)
    stage_e(6)
    stage_r(5)
    stage_h(5)
    stage_e(7)
    stage_r(6)
    stage_h(6)
    stage_g(5)
    stage_r(7)
    stage_g(6)
    stage_h(7)
    stage_g(7)
    stage_h2(5)
    stage_h2(6)
    stage_h2(7)
    for c in range(CHUNKS):
        stage_i(c)

    for j in range(2 * YS):
        column = fg[j, aux]
        real, imag = column[:128], column[128:]
        cols[j] = jnp.concatenate(
            [jnp.concatenate([real, imag], 1), jnp.concatenate([-imag, real], 1)], 0
        )

    def tile(i, carry):
        total = jnp.zeros((256, 256), F32)
        for j in range(2 * YS):
            rows = jnp.concatenate(
                [jnp.concatenate([fg[j, 2 * i + n, :128], fg[j, 2 * i + n, 128:]], 1) for n in range(2)], 0
            )
            total = total + matmul_nt(rows, cols[j])
        at = pl.ds(pl.multiple_of(i * 256, 256), 256)
        out[0, at, :] = total[:, :128]
        out[1, at, :] = total[:, 128:]
        return carry

    lax.fori_loop(0, CHUNKS // 2, tile, 0)

    for kind in range(KINDS):
        for c in range(CHUNKS if kind else CHUNKS // 2):
            move(kind, c).wait_send()


def local(orbital_coef, dftensor, shifted_index):
    nao, nemb = orbital_coef.shape[2:]
    depth = dftensor.shape[-1]
    tensor = dftensor.reshape(2, nao, nao, depth)
    unit = (2 * nemb, depth)
    return pl.pallas_call(
        kernel,
        out_shape=jax.ShapeDtypeStruct((2, 8 * nemb, nemb), F32),
        in_specs=[
            pl.BlockSpec(memory_space=pltpu.VMEM),
            pl.BlockSpec(memory_space=pl.ANY),
            pl.BlockSpec(memory_space=pltpu.SMEM),
        ],
        out_specs=pl.BlockSpec(memory_space=pltpu.VMEM),
        scratch_shapes=[
            pltpu.VMEM((SLOTS, 2, nao, ROWS, depth), BF16),
            pltpu.VMEM((nao // ROWS, ROWS, 2 * nao, depth), BF16),
            pltpu.VMEM((ROWS, nemb, depth), BF16),
            pltpu.VMEM((3, 2 * nemb, 128), F32),
            pltpu.VMEM((2, nemb, 2 * nao), BF16),
            pltpu.VMEM((2 * nemb, 2 * nao), BF16),
            pltpu.VMEM((2, nemb, nao, depth), BF16),
            pltpu.VMEM((CORES * ZS * XS, 2, nao // YS, nemb), BF16),
            pltpu.VMEM((YS, 2, nao // YS, nemb), BF16),
            pltpu.VMEM((CHUNKS, ZS * XS) + unit, BF16),
            pltpu.VMEM((CHUNKS, ZS * XS) + unit, F32),
            pltpu.VMEM((CHUNKS, ZS * XS) + unit, BF16),
            pltpu.VMEM((CHUNKS,) + unit, BF16),
            pltpu.VMEM((CHUNKS,) + unit, BF16),
            pltpu.VMEM((CHUNKS, XS) + unit, BF16),
            pltpu.VMEM((CHUNKS, XS) + unit, BF16),
            pltpu.VMEM((CHUNKS,) + unit, BF16),
            pltpu.VMEM((CHUNKS, nemb, depth), BF16),
            pltpu.VMEM((CHUNKS, nemb, depth), BF16),
            pltpu.VMEM((2 * YS, CHUNKS) + unit, BF16),
            pltpu.VMEM((2 * YS, 2 * nemb, 2 * depth), BF16),
            pltpu.SemaphoreType.DMA((SLOTS,)),
            pltpu.SemaphoreType.DMA((NKA + YS - 2,)),
            pltpu.SemaphoreType.DMA((NKA + YS - 2,)),
            pltpu.SemaphoreType.DMA((KINDS, CHUNKS)),
            pltpu.SemaphoreType.DMA((KINDS, CHUNKS)),
            pltpu.SemaphoreType.DMA,
        ],
        compiler_params=pltpu.CompilerParams(
            collective_id=0, has_side_effects=True, vmem_limit_bytes=67_000_000
        ),
    )(orbital_coef, tensor, shifted_index)


def solution(mesh):
    placed = (P(None, "ka", None, None), P(None, "ka", None, None, "aux"), P())
    return jax.shard_map(
        local, mesh=mesh, in_specs=placed, out_specs=P(None, "ka", "aux"), check_vma=False
    )
```

time: 102 us -> 89.9 us (0.88)
  Pallas kernels: 99.4 us -> 87.4 us
    pallas_call x1, Pallas kernels: 99.4 us -> 87.4 us  [local(): pl.pallas_call(kernel, out_shape=jax.ShapeDtypeStruct((2, 8 * nemb, nemb)...]
where the time goes in v1:
time: 89.9 us; the launch traced here: 89.7 us
  Pallas kernels  87.4 us (97%)
  local copies, waits for them, and re-layouts  2.26 us (3%)
    pallas_call x1, Pallas kernels, local(): pl.pallas_call(kernel, out_shape=jax.ShapeDtypeStruct((2, 8 * nemb, nemb)...  87.4 us
    unnamed x1, local copies, waits for them, and re-layouts  2.26 us

profile of v1, /device:TPU:0, one launch (start us, length us, event | category | flops | bytes accessed | tf_op | source)
XLA Modules:
  0.0 89.7 jit_solution(11845558417274149290)
XLA Ops:
  0.0 87.4 %shard_map.37 = f32[2,1024,128]{2,1,0:T(8,128)} custom-call(bf16[2,1,192,128]{3,2,1,0:T(8,128)(2,1)} %coef.1, bf16[2,192,192,128]{3,2,1,0:T(8,128)(2,1)} %bitcast.1, s32[16]{0:T(128)} %index.1), custom_call_target="tpu_custom_call" | custom-call | tf_op jit(solution)/shard_map/pallas_call | solution.py:393
  87.5 2.3 %copy.5 = f32[2,1024,128]{2,1,0:T(8,128)} copy(f32[2,1024,128]{2,1,0:T(8,128)} %shard_map.37) | data formatting | bytes 2097152

commit v2 on v1

--- a/solution.py
+++ b/solution.py
@@ -12,11 +12,11 @@
 ROWS = 16
 CHUNKS = 8
 SLOTS = 3
-PICK_AT = 8
+PICK_AT = 9
 UNROLL = 4
 CORES, ZS, XS, YS = 2, 4, 2, 4
 NKA = CORES * ZS * XS
-KINDS = 20
+KINDS = 17
 
 
 def matmul(left, right):
@@ -27,7 +27,7 @@
     return lax.dot_general(left, right, (((1,), (1,)), ((), ())), preferred_element_type=F32)
 
 
-def kernel(coef, tensor, index, out, blocks, turned, raw, w1f, w1, w2, half, cg, cs, away, mine, other, za, zb, zm, zp, xr, ra, rb, fg, cols,
+def kernel(coef, tensor, index, out, blocks, turned, raw, w1f, w1, w2, half, cg, cs, away, mine, other, za, zb, zm, zp, xr, fg, cols,
            lsem, gsend, grecv, dsend, drecv, local_sem):
     nao = coef.shape[2]
     part = nao // YS
@@ -43,7 +43,7 @@
     to_up = (x * CORES * ZS + up * CORES + core, aux)
     to_down = (x * CORES * ZS + down * CORES + core, aux)
     to_y_up, to_y_down = (ka, xh * YS + y_up), (ka, xh * YS + y_down)
-    to_out = (lax.rem(ka + CORES * ZS, XS * CORES * ZS), aux_far)
+    to_far = (ka, aux_far)
     x_other = 1 - x
 
     def load(i):
@@ -55,7 +55,7 @@
     barrier = pltpu.get_barrier_semaphore()
     to_ka = [(lax.rem(ka + n, NKA), aux) for n in range(1, NKA)]
     to_ys = [(ka, xh * YS + lax.rem(y + n, YS)) for n in range(1, YS)]
-    partners = to_ka + to_ys + [to_out]
+    partners = to_ka + to_ys + [to_far]
     for partner in partners:
         pl.semaphore_signal(barrier, inc=1, device_id=partner, device_id_type=MESH)
 
@@ -182,13 +182,7 @@
             return one(other.at[c, z * 2 + x_other], xr.at[c], to_x)
         low, high = pl.ds(0, 128), pl.ds(128, 128)
         if kind == 8:
-            return one(fg.at[aux, c, low], ra.at[c], to_x)
-        if kind == 17:
-            return one(fg.at[aux, c, high], rb.at[c], to_out)
-        if kind == 18:
-            return one(ra.at[c], fg.at[aux, c, low], to_out)
-        if kind == 19:
-            return one(rb.at[c], fg.at[aux_far, c, high], to_x)
+            return one(fg.at[aux, c], fg.at[aux, c], to_far)
         if kind in (9, 10):
             return one(fg.at[aux, c], fg.at[aux, c], to_y_up if kind == 9 else to_y_down)
         if kind in (11, 12):
@@ -237,17 +231,11 @@
         move(7, c).wait_recv()
         q = z * 2 + x
         add(fg.at[aux, c], (mine.at[c, q], other.at[c, q], zm.at[c, x], zp.at[c, x], xr.at[c]), 1 / (CORES * ZS * XS))
-        for kind in (8, 17, 9, 10):
-            move(kind, c).start()
-
-    def stage_r(c):
-        for wait_kind, kind in ((8, 18), (17, 19)):
-            move(wait_kind, c).wait_recv()
+        for kind in (8, 9, 10):
             move(kind, c).start()
 
     def stage_g(c):
-        move(18, c).wait_recv()
-        move(19, c).wait_recv()
+        move(8, c).wait_recv()
         move(11, c).start()
         move(12, c).start()
 
@@ -269,87 +257,80 @@
     pair_mine(0)
     second(0, 1)
     pair_away(1)
+    second(1, 2)
     pair_mine(1)
     wait_core(0)
     stage_a(0)
+    stage_a2(0)
+    second(2, 4)
     stage_a(1)
-    second(1, 3)
-    stage_a2(0)
-    second(3, 4)
+    second(4, 5)
     wait_core(1)
-    second(4, 5)
+    second(5, 6)
+    stage_a(2)
+    second(6, 7)
+    stage_b(0)
+    second(7, 10)
     stage_a2(1)
-    second(5, 6)
-    stage_b(0)
-    second(6, 8)
+    second(10, 12)
     stage_b(1)
-    second(8, 12)
-    stage_a(2)
     pair_away(2)
+    pair_mine(2)
     stage_a2(2)
+    stage_b(2)
     pair_away(3)
     stage_d(0)
-    pair_mine(2)
+    pair_mine(3)
+    wait_core(2)
     stage_a(3)
     stage_d(1)
-    pair_mine(3)
-    wait_core(2)
     stage_a(4)
-    stage_b(2)
+    wait_core(3)
     stage_e(0)
-    wait_core(3)
+    stage_a2(3)
+    stage_d(2)
     stage_a2(4)
     stage_e(1)
-    stage_r(0)
-    stage_a2(3)
     stage_b(3)
+    stage_h(0)
     stage_b(4)
-    stage_h(0)
-    stage_r(1)
-    stage_d(2)
+    stage_e(2)
     stage_h(1)
+    stage_a(5)
     stage_g(0)
+    stage_a2(5)
+    stage_d(3)
     stage_g(1)
-    stage_a(5)
-    stage_e(2)
-    stage_a2(5)
+    stage_h(2)
+    stage_a(6)
+    stage_d(4)
+    stage_a2(6)
+    stage_g(2)
     stage_h2(0)
-    stage_d(3)
-    stage_a(6)
-    stage_h2(1)
-    stage_d(4)
-    stage_r(2)
-    stage_a2(6)
-    stage_h(2)
     stage_b(5)
     stage_e(3)
+    stage_h2(1)
+    stage_a(7)
     stage_e(4)
-    stage_a(7)
-    stage_g(2)
     stage_b(6)
-    stage_r(3)
+    stage_h2(2)
+    stage_a2(7)
     stage_h(3)
-    stage_r(4)
-    stage_a2(7)
-    stage_h(4)
     stage_d(5)
     stage_g(3)
-    stage_h2(2)
+    stage_b(7)
+    stage_h(4)
     stage_g(4)
-    stage_b(7)
     stage_d(6)
     stage_e(5)
     stage_h2(3)
     stage_d(7)
+    stage_e(6)
     stage_h2(4)
-    stage_e(6)
-    stage_r(5)
     stage_h(5)
     stage_e(7)
-    stage_r(6)
     stage_h(6)
     stage_g(5)
-    stage_r(7)
     stage_g(6)
     stage_h(7)
     stage_g(7)
@@ -417,8 +398,6 @@
             pltpu.VMEM((CHUNKS, XS) + unit, BF16),
             pltpu.VMEM((CHUNKS, XS) + unit, BF16),
             pltpu.VMEM((CHUNKS,) + unit, BF16),
-            pltpu.VMEM((CHUNKS, nemb, depth), BF16),
-            pltpu.VMEM((CHUNKS, nemb, depth), BF16),
             pltpu.VMEM((2 * YS, CHUNKS) + unit, BF16),
             pltpu.VMEM((2 * YS, 2 * nemb, 2 * depth), BF16),
             pltpu.SemaphoreType.DMA((SLOTS,)),

time: 89.9 us -> 86 us (0.957)
  Pallas kernels: 87.4 us -> 83.6 us
    pallas_call x1, Pallas kernels: 87.4 us -> 83.6 us  [local(): pl.pallas_call(kernel, out_shape=jax.ShapeDtypeStruct((2, 8 * nemb, nemb)...]
where the time goes in v2:
time: 86 us; the launch traced here: 85.9 us
  Pallas kernels  83.6 us (97%)
  local copies, waits for them, and re-layouts  2.26 us (3%)
    pallas_call x1, Pallas kernels, local(): pl.pallas_call(kernel, out_shape=jax.ShapeDtypeStruct((2, 8 * nemb, nemb)...  83.6 us
    unnamed x1, local copies, waits for them, and re-layouts  2.26 us

profile of v2, /device:TPU:0, one launch (start us, length us, event | category | flops | bytes accessed | tf_op | source)
XLA Modules:
  0.0 85.9 jit_solution(11734797290104492157)
XLA Ops:
  0.0 83.6 %shard_map.37 = f32[2,1024,128]{2,1,0:T(8,128)} custom-call(bf16[2,1,192,128]{3,2,1,0:T(8,128)(2,1)} %coef.1, bf16[2,192,192,128]{3,2,1,0:T(8,128)(2,1)} %bitcast.1, s32[16]{0:T(128)} %index.1), custom_call_target="tpu_custom_call" | custom-call | tf_op jit(solution)/shard_map/pallas_call | solution.py:374
  83.6 2.3 %copy.5 = f32[2,1024,128]{2,1,0:T(8,128)} copy(f32[2,1024,128]{2,1,0:T(8,128)} %shard_map.37) | data formatting | bytes 2097152

commit v3 on v2

--- a/solution.py
+++ b/solution.py
@@ -13,7 +13,7 @@
 CHUNKS = 8
 SLOTS = 3
 PICK_AT = 9
-UNROLL = 4
+UNROLL = 8
 CORES, ZS, XS, YS = 2, 4, 2, 4
 NKA = CORES * ZS * XS
 KINDS = 17

time: 86 us -> 85.3 us (level)
  no operation moved by 1% of the time
where the time goes in v3:
time: 85.3 us; the launch traced here: 85.1 us
  Pallas kernels  82.8 us (97%)
  local copies, waits for them, and re-layouts  2.26 us (3%)
    pallas_call x1, Pallas kernels, local(): pl.pallas_call(kernel, out_shape=jax.ShapeDtypeStruct((2, 8 * nemb, nemb)...  82.8 us
    unnamed x1, local copies, waits for them, and re-layouts  2.26 us

profile of v3, /device:TPU:0, one launch (start us, length us, event | category | flops | bytes accessed | tf_op | source)
XLA Modules:
  0.0 85.1 jit_solution(3066255277650925759)
XLA Ops:
  0.0 82.8 %shard_map.37 = f32[2,1024,128]{2,1,0:T(8,128)} custom-call(bf16[2,1,192,128]{3,2,1,0:T(8,128)(2,1)} %coef.1, bf16[2,192,192,128]{3,2,1,0:T(8,128)(2,1)} %bitcast.1, s32[16]{0:T(128)} %index.1), custom_call_target="tpu_custom_call" | custom-call | tf_op jit(solution)/shard_map/pallas_call | solution.py:374
  82.8 2.3 %copy.5 = f32[2,1024,128]{2,1,0:T(8,128)} copy(f32[2,1024,128]{2,1,0:T(8,128)} %shard_map.37) | data formatting | bytes 2097152

commit v4 on v3

--- a/solution.py
+++ b/solution.py
@@ -359,7 +359,7 @@
         out[1, at, :] = total[:, 128:]
         return carry
 
-    lax.fori_loop(0, CHUNKS // 2, tile, 0)
+    lax.fori_loop(0, CHUNKS // 2, tile, 0, unroll=2)
 
     for kind in range(KINDS):
         for c in range(CHUNKS if kind else CHUNKS // 2):

time: 85.3 us -> 84.9 us (level)
  no operation moved by 1% of the time
where the time goes in v4:
time: 84.9 us; the launch traced here: 84.7 us
  Pallas kernels  82.4 us (97%)
  local copies, waits for them, and re-layouts  2.26 us (3%)
    pallas_call x1, Pallas kernels, local(): pl.pallas_call(kernel, out_shape=jax.ShapeDtypeStruct((2, 8 * nemb, nemb)...  82.4 us
    unnamed x1, local copies, waits for them, and re-layouts  2.26 us

profile of v4, /device:TPU:0, one launch (start us, length us, event | category | flops | bytes accessed | tf_op | source)
XLA Modules:
  0.0 84.7 jit_solution(2314433991665165744)
XLA Ops:
  0.0 82.4 %shard_map.37 = f32[2,1024,128]{2,1,0:T(8,128)} custom-call(bf16[2,1,192,128]{3,2,1,0:T(8,128)(2,1)} %coef.1, bf16[2,192,192,128]{3,2,1,0:T(8,128)(2,1)} %bitcast.1, s32[16]{0:T(128)} %index.1), custom_call_target="tpu_custom_call" | custom-call | tf_op jit(solution)/shard_map/pallas_call | solution.py:374
  82.4 2.3 %copy.5 = f32[2,1024,128]{2,1,0:T(8,128)} copy(f32[2,1024,128]{2,1,0:T(8,128)} %shard_map.37) | data formatting | bytes 2097152
